TPU v7x, 256 devices: a whole 4x4x8 slice. The times are simulated.
256 devices in a mesh: row: 8 (over y, core), col: 32 (over x, z).
Axes of the slice: x: 4, y: 4, z: 8, core: 2. Of those that a mesh axis runs over, the one named last changes fastest.
Arguments:
- kkt: float32 [8192, 8192], P('row', 'col'), may hold values from -4 to 4, as said below
- swaps: int32 [2, 2, 128], replicated, may hold values from 0 to 8191, as said below
- inverses: float32 [2, 256, 256], replicated
- pivots: float32 [2, 256], replicated, may hold values from -0.12 to 0.12
- couplings: float32 [2, 256], replicated, may hold values from -0.12 to 0.12
- pattern: int32 [2, 256], replicated, may hold values from 0 to 1, as said below
Outputs:
- factored: float32 [8192, 8192], P('row', 'col')
Inputs may be any that keep to these rules, and one draw needn't show every extreme that they name: For panel k, swaps[k, 0, :] holds 128 distinct rows among k * 256 to k * 256 + 255, both ends of that range among them, and swaps[k, 1, :] holds 128 distinct rows among (k + 1) * 256 to 8191, both ends of that range among them. pattern[k, i] = 1 makes rows i and i + 1 one 2 x 2 block of D; no two neighbouring entries are both 1 and the last entry is 0. kkt is the stored order of a symmetric matrix.
All inputs are finite; a program needn't handle non-finite values.
Results may differ from a plain program's by a relative error of at most 0.00014.
Values sent between devices are 32-bit elements; how exact they have to be, the bound alone decides.
A program may use at most 64 MiB of HBM per device.

v0:
```python
import jax
import jax.numpy as jnp
from jax import lax
from jax.sharding import Mesh
from jax.sharding import PartitionSpec as P

COL = ("col_0", "col_1")
HI = lax.Precision.HIGHEST


def tdot(a, b):
    return lax.dot_general(
        a, b, (((0,), (0,)), ((), ())), precision=HI, preferred_element_type=jnp.float32
    )


def swapped(rows, lead, partner):
    to_partner = rows[:, None] == lead[None, :]
    to_lead = rows[:, None] == partner[None, :]
    moved = jnp.sum(
        jnp.where(to_partner, partner[None, :], 0) + jnp.where(to_lead, lead[None, :], 0), axis=1
    )
    return jnp.where(jnp.any(to_partner | to_lead, axis=1), moved, rows)


def plan(swaps, tile, row_groups, dtype=jnp.float32):
    width = tile // row_groups
    count = swaps.shape[2]
    partner = swaps[:, 1, :].reshape(-1)
    top = jnp.arange(2 * tile, dtype=jnp.int32)
    rows = jnp.concatenate([top, partner])
    source = swapped(swapped(rows, swaps[1, 0], swaps[1, 1]), swaps[0, 0], swaps[0, 1])
    repeated = jnp.any(swaps[0, 1][:, None] == swaps[1, 1][None, :], axis=1)
    valid = jnp.concatenate([~repeated, jnp.ones((count,), bool)]) & (partner >= 2 * tile)
    sliced = source.reshape(3, row_groups, width).transpose(1, 0, 2)
    return (rows, source, sliced, jnp.where(valid, partner, -1))


def hits(rows, first, tile):
    return (rows[:, None] == first + jnp.arange(tile, dtype=jnp.int32)[None, :]).astype(jnp.float32)


def along_d(lower_t, pivot, coupling, pattern):
    links = coupling * pattern.astype(jnp.float32)
    zero = jnp.zeros((1, lower_t.shape[1]), lower_t.dtype)
    after = jnp.concatenate([lower_t[1:], zero], axis=0)
    before = jnp.concatenate([zero, lower_t[:-1]], axis=0)
    links_before = jnp.concatenate([jnp.zeros((1,), links.dtype), links[:-1]])
    return lower_t * pivot[:, None] + after * links[:, None] + before * links_before[:, None]


def exchange(picked, moves, tile, row_groups, x_size):
    width = tile // row_groups
    row_index = lax.axis_index("row")
    z_index = lax.axis_index("col_1")
    piece = lax.psum_scatter(picked, "row", scatter_dimension=0, tiled=False)
    strip = lax.all_gather(piece, "row")
    mine = lax.psum(jnp.where(z_index == row_index, strip, 0.0), "col_1")
    wide = lax.all_gather(mine, "col_0")
    part = jnp.dot(piece, moves, precision=HI, preferred_element_type=jnp.float32)
    t0, t1, tp = (part[:width], part[width : 2 * width], part[2 * width :])
    corner = jnp.stack(
        [
            t0[:, 2 * tile :],
            t1[:, 2 * tile :],
            tp[:, 2 * tile :],
            t0[:, tile : 2 * tile],
            t0[:, :tile],
            t1[:, tile : 2 * tile],
        ]
    )
    corner = lax.all_gather(lax.psum(corner, COL), "row")
    return (strip, wide, corner)


def shards(kkt, swaps, inverses, pivots, couplings, pattern):
    tile = inverses.shape[1]
    row_groups = lax.axis_size("row")
    x_size = lax.axis_size("col_0")
    z_size = lax.axis_size("col_1")
    row_index = lax.axis_index("row")
    col_index = lax.axis_index(COL)
    rows, source, sliced, partner = plan(swaps, tile, row_groups)
    flat = sliced.reshape(-1)
    owned = flat // tile % row_groups == row_index
    taken = jnp.take(kkt, flat // tile // row_groups * tile + flat % tile, axis=0)
    picked = jnp.where(owned[:, None], taken, 0.0).reshape(row_groups, -1, tile)
    moves = hits(source, col_index * tile, tile).T
    strip, wide, corner = exchange(picked, moves, tile, row_groups, x_size)

    def ordered(piece):
        return piece.reshape(row_groups, 3, -1, tile).transpose(1, 0, 2, 3).reshape(-1, tile)

    corner = corner.transpose(1, 0, 2, 3).reshape(6, tile, tile)
    to_partner = corner[0:3].reshape(3 * tile, tile)
    block_01, block_00, block_11 = (corner[3], corner[4], corner[5])
    tiles = [row_index + row_groups * slot for slot in range(x_size)] + [col_index]
    strips = [ordered(wide[slot]) for slot in range(x_size)] + [ordered(strip)]
    marks = [hits(partner, index * tile, tile) for index in tiles]
    keep = [1.0 - jnp.sum(mark, axis=0) for mark in marks]
    fixed = [
        strips[n] * keep[n][None, :]
        + jnp.dot(to_partner, marks[n], precision=HI, preferred_element_type=jnp.float32)
        for n in range(x_size + 1)
    ]
    upper = [jnp.where(tiles[n] == 1, block_01, fixed[n][:tile]) for n in range(x_size + 1)]
    low0 = [jnp.where(tiles[n] > 0, tdot(inverses[0], upper[n]), 0.0) for n in range(x_size + 1)]
    low0_1 = tdot(inverses[0], block_01)
    scaled0_1 = along_d(low0_1, pivots[0], couplings[0], pattern[0])
    scaled0 = along_d(low0[-1], pivots[0], couplings[0], pattern[0])
    low1 = [
        jnp.where(
            tiles[n] > 1,
            tdot(inverses[1], fixed[n][tile : 2 * tile] - tdot(scaled0_1, low0[n])),
            0.0,
        )
        for n in range(x_size + 1)
    ]
    scaled1 = along_d(low1[-1], pivots[1], couplings[1], pattern[1])
    outs = []
    for n in range(x_size):
        base = kkt[n * tile : (n + 1) * tile] * keep[n][:, None] * keep[-1][None, :]
        base = base + tdot(marks[n], fixed[-1][2 * tile :])
        base = base + tdot(fixed[n][2 * tile :] * keep[n][None, :], marks[-1])
        value = base - tdot(low0[n], scaled0) - tdot(low1[n], scaled1)
        value = jnp.where(tiles[n] == 0, scaled0, value)
        value = jnp.where(tiles[n] == 1, scaled1, value)
        at_0 = jnp.where(tiles[n] == 0, block_00, low0[n].T)
        at_1 = jnp.where(tiles[n] == 0, scaled0_1, low1[n].T)
        at_1 = jnp.where(tiles[n] == 1, block_11 - tdot(low0_1, scaled0_1), at_1)
        value = jnp.where(col_index == 0, at_0, value)
        value = jnp.where(col_index == 1, at_1, value)
        outs.append(value)
    return jnp.concatenate(outs, axis=0)


def solution(mesh):
    z_size = mesh.shape["row"]
    finer = Mesh(mesh.devices.reshape(mesh.shape["row"], -1, z_size), ("row", "col_0", "col_1"))
    in_specs = (P("row", COL), P(), P(), P(), P(), P())
    return jax.shard_map(
        shards, mesh=finer, in_specs=in_specs, out_specs=P("row", COL), check_vma=False
    )
```

profile of v0, /device:TPU:1, one launch (start us, length us, event | category | flops | bytes accessed | tf_op | source)
XLA Modules:
  0.0 369.6 jit_solution(7685777161819229525)
XLA Ops:
  6.5 0.8 slice_bitcast_fusion.9
  7.3 0.7 slice.199
  8.0 0.3 fusion.38
  8.3 0.3 fusion.33
  8.6 0.3 fusion.39
  8.9 0.3 fusion.35
  9.6 3.3 gather_fusion
  12.9 1.2 select_select_fusion
  14.2 35.9 %reduce-scatter.2.cloned.1.call-done = f32[1,96,256]{2,1,0:T(8,128)} async-done(((f32[8,96,256]{2,1,0:T(8,128)}), f32[1,96,256]{2,1,0:T(8,128)}) %reduce-scatter.2.cloned.1.call-update) | async-done | bytes 98320 | tf_op jit(solution)/shard_map/reduce_scatter | solution.py:56
  50.1 1.5 fusion.17
  51.6 0.7 copy-done.4
  52.4 16.4 %all_gather.17 = f32[8,96,256]{2,1,0:T(8,128)S(1)} all-gather(f32[1,96,256]{2,1,0:T(8,128)} %reduce-scatter.2.cloned.1.call-done), channel_id=1, replica_groups=mesh['row'=8,'col_0'=4,'col_1'=8] {'row'}, dimensions={0}, use_global_device_ids=true | all-gather | bytes 884736 | tf_op jit(solution)/shard_map/all_gather | solution.py:57
  68.8 1.0 select_bitcast_fusion
  69.8 124.7 %all-reduce.10.cloned.1.call-done = f32[1,6,32,256]{3,2,1,0:T(8,128)} async-done(((f32[1,6,32,256]{3,2,1,0:T(8,128)}), f32[1,6,32,256]{3,2,1,0:T(8,128)}) %all-reduce.10.cloned.1.call-update) | async-done | bytes 196624 | tf_op jit(solution)/shard_map/psum | solution.py:72
  194.5 0.2 all-gather.5.cloned.1.call-start
  195.0 0.2 fusion.40
  195.3 73.7 %all-reduce.12.cloned.1.call-done = f32[1,8,96,256]{3,2,1,0:T(8,128)} async-done(((f32[1,8,96,256]{3,2,1,0:T(8,128)}), f32[1,8,96,256]{3,2,1,0:T(8,128)}) %all-reduce.12.cloned.1.call-update) | async-done | bytes 786448 | tf_op jit(solution)/shard_map/psum | solution.py:58
  269.2 31.6 %all-gather.3.cloned.1.call-done = f32[8,6,32,256]{3,2,1,0:T(8,128)} async-done(((f32[1,6,32,256]{3,2,1,0:T(8,128)}), f32[8,6,32,256]{3,2,1,0:T(8,128)}) %all-gather.3.cloned.1.call-update) | async-done | bytes 1572880 | tf_op jit(solution)/shard_map/all_gather | solution.py:72
  300.8 1.5 copy.51
  302.4 0.8 fusion.125
  303.4 0.6 fusion.55
  304.0 0.6 convolution_add_fusion.3
  304.6 0.6 convolution_select_fusion.7
  305.3 0.2 multiply_add_fusion
  305.5 0.6 convolution_subtract_fusion.11
  306.1 0.6 fusion.8
  306.9 0.4 copy-done
  307.3 1.2 convolution_add_fusion.6
  308.5 0.5 convolution_add_fusion.8
  309.0 0.5 convolution_add_fusion.10
  309.5 0.5 convolution_add_fusion.12
  310.0 0.6 convolution_subtract_fusion.13
  310.6 33.6 %all-gather.5.cloned.1.call-done = f32[4,8,96,256]{3,2,1,0:T(8,128)} async-done(((f32[1,8,96,256]{3,2,1,0:T(8,128)}), f32[4,8,96,256]{3,2,1,0:T(8,128)}) %all-gather.5.cloned.1.call-update) | async-done | bytes 3145744 | tf_op jit(solution)/shard_map/all_gather | solution.py:59
  344.2 2.2 fusion.124
  346.5 0.6 convolution_add_fusion.2
  347.2 0.6 convolution_add_fusion.1
  347.9 0.6 convolution_add_fusion
  348.6 0.6 convolution_add_fusion.4
  349.2 0.4 copy-done.2
  349.6 0.4 convolution_add_fusion.5
  350.0 0.6 convolution_select_fusion.1
  350.6 0.6 convolution_subtract_fusion.2
  351.2 0.4 convolution_add_fusion.7
  351.7 0.6 convolution_select_fusion.3
  352.3 0.8 convolution_subtract_fusion.5
  353.1 0.4 convolution_subtract_fusion.1
  353.5 0.4 convolution_subtract_fusion.4
  353.9 0.4 convolution_add_fusion.9
  354.3 0.6 convolution_select_fusion.5
  354.9 0.6 convolution_subtract_fusion.8
  355.6 0.4 convolution_subtract_fusion.7
  355.9 0.4 convolution_add_fusion.11
  356.4 0.6 bitcast_select_fusion.3
  357.0 0.6 convolution_subtract_fusion.12
  357.6 0.4 convolution_subtract_fusion.10
  358.0 0.6 convolution_select_fusion
  358.6 0.6 convolution_select_fusion.2
  359.2 0.6 convolution_select_fusion.4
  359.8 0.6 convolution_select_fusion.8
  360.4 0.4 fusion.16
  360.8 0.4 fusion.14
  361.2 0.4 fusion.12
  361.6 0.4 fusion.10
  362.1 1.0 pad_maximum_fusion
  (67 shorter events, 2.1 us)
Async XLA Ops:
  6.5 43.5 %reduce-scatter.2.cloned.1.call-start = ((), (), s32[]{:S(2)}) async-start(), calls=%async_computation.1 | async-start | bytes 884736 | tf_op jit(solution)/shard_map/reduce_scatter | solution.py:56
  14.1 180.4 %all-reduce.10.cloned.1.call-start = ((), (), s32[]{:S(2)}) async-start(), calls=%async_computation.2 | async-start | bytes 393216 | tf_op jit(solution)/shard_map/psum | solution.py:72
  51.6 0.7 copy-start.4
  52.3 142.9 %copy-start.5 = (s32[2,256]{1,0:T(2,128)S(1)}, s32[2,256]{1,0:T(2,128)}, u32[]{:S(2)}) copy-start(s32[2,256]{1,0:T(2,128)} %param.11) | copy-start | bytes 6148
  52.3 142.9 %copy-start.6 = (f32[2,256]{1,0:T(2,128)S(1)}, f32[2,256]{1,0:T(2,128)}, u32[]{:S(2)}) copy-start(f32[2,256]{1,0:T(2,128)} %param.10) | copy-start | bytes 6148
  52.4 216.6 %all-reduce.12.cloned.1.call-start = ((), (), s32[]{:S(2)}) async-start(), calls=%async_computation.4 | async-start | bytes 1572864 | tf_op jit(solution)/shard_map/psum | solution.py:58
  68.8 200.2 %copy-start.7 = (f32[2,256]{1,0:T(2,128)S(1)}, f32[2,256]{1,0:T(2,128)}, u32[]{:S(2)}) copy-start(f32[2,256]{1,0:T(2,128)} %param.9) | copy-start | bytes 6148
  69.8 231.1 %all-gather.3.cloned.1.call-start = ((), (), s32[]{:S(2)}) async-start(), calls=%async_computation.3 | async-start | bytes 1769472 | tf_op jit(solution)/shard_map/all_gather | solution.py:72
  194.5 149.6 %all-gather.5.cloned.1.call-start = ((), (), s32[]{:S(2)}) async-start(), calls=%async_computation.5 | async-start | bytes 3932160 | tf_op jit(solution)/shard_map/all_gather | solution.py:59
  302.4 1.0 copy-start.1
  306.1 1.2 copy-start
  348.6 1.0 copy-start.2
  354.9 1.5 copy-start.3
Sparse Core Ops, SparseCore 0:
  14.2 35.8 reduce-scatter.1
  53.5 140.9 all-reduce.9
  196.8 72.0 all-reduce.11
  270.6 30.1 all-gather.2
  302.5 41.6 all-gather.4
where the time goes:
time: 370 us
  waiting for transfers between devices  300 us (81%)
  matrix products  22.2 us (6%)
  blocking collectives  16.4 us (4%)
  between operations  13.9 us (4%)
  local copies, waits for them, and re-layouts  11.6 us (3%)
  other arithmetic  5.64 us (2%)
    psum x1, waiting for transfers between devices, exchange(): corner = lax.all_gather(lax.psum(corner, COL), 'row')  125 us
    psum x1, waiting for transfers between devices, exchange(): mine = lax.psum(jnp.where(z_index == row_index, strip, 0.0), 'col_1')  73.7 us
    reduce_scatter x1, waiting for transfers between devices, exchange(): piece = lax.psum_scatter(picked, 'row', scatter_dimension=0, tiled=False)  35.9 us
    all_gather x1, waiting for transfers between devices, exchange(): wide = lax.all_gather(mine, 'col_0')  33.6 us
    all_gather x1, waiting for transfers between devices, exchange(): corner = lax.all_gather(lax.psum(corner, COL), 'row')  31.6 us
    dot_general x33, matrix products, tdot(): lax.dot_general(a, b, (((0,), (0,)), ((), ())), precision=HI, preferred_e...  17.9 us
    all_gather x1, blocking collectives, exchange(): strip = lax.all_gather(piece, 'row')  16.4 us
  transfers between devices with their start and end apart: 5, of which 5 were waited for; matrix products, arithmetic and copies ran while one was open for 3% of the time, Pallas kernels for 0%

commit v1 on v0

--- a/solution.py
+++ b/solution.py
@@ -6,6 +6,11 @@
 
 COL = ("col_0", "col_1")
 HI = lax.Precision.HIGHEST
+
+
+def axis_by_axis(array, axis_one, axis_two):
+    partial = lax.psum(array, axis_one)
+    return lax.psum(partial, axis_two)
 
 
 def tdot(a, b):
@@ -69,7 +74,7 @@
             t1[:, tile : 2 * tile],
         ]
     )
-    corner = lax.all_gather(lax.psum(corner, COL), "row")
+    corner = lax.all_gather(axis_by_axis(corner, "col_1", "col_0"), "row")
     return (strip, wide, corner)
 
 

time: 370 us -> 290 us (0.78)
  waiting for transfers between devices: 300 us -> 220 us
    psum x2, waiting for transfers between devices: 198 us -> 120 us  [the longest x1 70.6 us: axis_by_axis(): partial = lax.psum(array, axis_one)]
where the time goes in v1:
time: 290 us
  waiting for transfers between devices  220 us (76%)
  matrix products  22.2 us (8%)
  blocking collectives  16.4 us (6%)
  between operations  13.9 us (5%)
  local copies, waits for them, and re-layouts  11 us (4%)
  other arithmetic  5.64 us (2%)
    psum x1, waiting for transfers between devices, axis_by_axis(): partial = lax.psum(array, axis_one)  70.6 us
    psum x1, waiting for transfers between devices, axis_by_axis(): return lax.psum(partial, axis_two)  49.7 us
    reduce_scatter x1, waiting for transfers between devices, exchange(): piece = lax.psum_scatter(picked, 'row', scatter_dimension=0, tiled=False)  35.9 us
    all_gather x1, waiting for transfers between devices, exchange(): wide = lax.all_gather(mine, 'col_0')  33.6 us
    all_gather x1, waiting for transfers between devices, exchange(): corner = lax.all_gather(axis_by_axis(corner, 'col_1', 'col_0'), 'row')  30.6 us
    dot_general x33, matrix products, tdot(): lax.dot_general(a, b, (((0,), (0,)), ((), ())), precision=HI, preferred_e...  17.9 us
    all_gather x1, blocking collectives, exchange(): strip = lax.all_gather(piece, 'row')  16.4 us
  transfers between devices with their start and end apart: 5, of which 5 were waited for; matrix products, arithmetic and copies ran while one was open for 3% of the time, Pallas kernels for 0%

profile of v1, /device:TPU:1, one launch (start us, length us, event | category | flops | bytes accessed | tf_op | source)
XLA Modules:
  0.0 289.9 jit_solution(5662673322591076577)
XLA Ops:
  6.5 0.8 slice_bitcast_fusion.9
  7.3 0.7 slice.199
  8.0 0.3 fusion.38
  8.3 0.3 fusion.33
  8.6 0.3 fusion.39
  8.9 0.3 fusion.35
  9.6 3.3 %gather_fusion = f32[768,256]{1,0:T(8,128)S(1)} fusion(f32[1024,256]{1,0:T(8,128)} %param.6, s32[1024]{0:T(1024)S(1)} %pad_clamp_fusion), kind=kCustom, calls=%fused_computation | custom fusion | bytes 1575936 | tf_op jit(solution)/shard_map/jit(_take)/gather | solution.py:91
  12.9 1.2 select_select_fusion
  14.2 35.9 %reduce-scatter.2.cloned.1.call-done = f32[1,96,256]{2,1,0:T(8,128)} async-done(((f32[8,96,256]{2,1,0:T(8,128)}), f32[1,96,256]{2,1,0:T(8,128)}) %reduce-scatter.2.cloned.1.call-update) | async-done | bytes 98320 | tf_op jit(solution)/shard_map/reduce_scatter | solution.py:61
  50.1 1.5 fusion.17
  51.6 16.4 %all_gather.17 = f32[8,96,256]{2,1,0:T(8,128)S(1)} all-gather(f32[1,96,256]{2,1,0:T(8,128)} %reduce-scatter.2.cloned.1.call-done), channel_id=1, replica_groups=mesh['row'=8,'col_0'=4,'col_1'=8] {'row'}, dimensions={0}, use_global_device_ids=true | all-gather | bytes 884736 | tf_op jit(solution)/shard_map/all_gather | solution.py:62
  68.1 1.0 select_bitcast_fusion
  69.1 70.6 %all-reduce.13.cloned.1.call-done = (f32[6,32,256]{2,1,0:T(8,128)}, f32[1,8,96,256]{3,2,1,0:T(8,128)}) async-done(((f32[6,32,256]{2,1,0:T(8,128)}, f32[1,8,96,256]{3,2,1,0:T(8,128)}), (f32[6,32,256]{2,1,0:T(8,128)}, f32[1,8,96,256]{3,2,1,0:T(8,128)})) %all-reduce.13.cloned.1.call-update) | async-done | bytes 983056 | tf_op jit(solution)/shard_map/psum | solution.py:12
  139.7 49.7 %all-reduce.11.cloned.1.call-done = f32[1,6,32,256]{3,2,1,0:T(8,128)} async-done(((f32[1,6,32,256]{3,2,1,0:T(8,128)}), f32[1,6,32,256]{3,2,1,0:T(8,128)}) %all-reduce.11.cloned.1.call-update) | async-done | bytes 196624 | tf_op jit(solution)/shard_map/psum | solution.py:13
  189.5 0.2 all-gather.5.cloned.1.call-start
  190.0 0.2 fusion.40
  190.5 30.6 %all-gather.3.cloned.1.call-done = f32[8,6,32,256]{3,2,1,0:T(8,128)} async-done(((f32[1,6,32,256]{3,2,1,0:T(8,128)}), f32[8,6,32,256]{3,2,1,0:T(8,128)}) %all-gather.3.cloned.1.call-update) | async-done | bytes 1572880 | tf_op jit(solution)/shard_map/all_gather | solution.py:77
  221.0 1.5 copy.51
  222.7 0.8 fusion.125
  223.4 0.2 copy-done.1
  223.6 0.6 fusion.55
  224.2 0.6 convolution_add_fusion.3
  224.8 0.6 convolution_select_fusion.7
  225.5 0.2 multiply_add_fusion
  225.7 0.6 convolution_subtract_fusion.11
  226.3 0.6 fusion.8
  227.1 0.4 copy-done
  227.5 1.2 convolution_add_fusion.6
  228.7 0.5 convolution_add_fusion.8
  229.2 0.5 convolution_add_fusion.10
  229.7 0.5 convolution_add_fusion.12
  230.2 0.6 convolution_subtract_fusion.13
  230.8 33.6 %all-gather.5.cloned.1.call-done = f32[4,8,96,256]{3,2,1,0:T(8,128)} async-done(((f32[1,8,96,256]{3,2,1,0:T(8,128)}), f32[4,8,96,256]{3,2,1,0:T(8,128)}) %all-gather.5.cloned.1.call-update) | async-done | bytes 3145744 | tf_op jit(solution)/shard_map/all_gather | solution.py:64
  264.4 2.2 fusion.124
  266.7 0.6 convolution_add_fusion.2
  267.4 0.6 convolution_add_fusion.1
  268.1 0.6 convolution_add_fusion
  268.8 0.6 convolution_add_fusion.4
  269.4 0.4 copy-done.2
  269.8 0.4 convolution_add_fusion.5
  270.2 0.6 convolution_select_fusion.1
  270.8 0.6 convolution_subtract_fusion.2
  271.4 0.4 convolution_add_fusion.7
  271.9 0.6 convolution_select_fusion.3
  272.5 0.8 convolution_subtract_fusion.5
  273.3 0.4 convolution_subtract_fusion.1
  273.7 0.4 convolution_subtract_fusion.4
  274.1 0.4 convolution_add_fusion.9
  274.6 0.6 convolution_select_fusion.5
  275.2 0.6 convolution_subtract_fusion.8
  275.8 0.4 convolution_subtract_fusion.7
  276.2 0.4 convolution_add_fusion.11
  276.6 0.6 bitcast_select_fusion.3
  277.2 0.6 convolution_subtract_fusion.12
  277.8 0.4 convolution_subtract_fusion.10
  278.2 0.6 convolution_select_fusion
  278.8 0.6 convolution_select_fusion.2
  279.4 0.6 convolution_select_fusion.4
  280.0 0.6 convolution_select_fusion.8
  280.6 0.4 fusion.16
  281.1 0.4 fusion.14
  281.5 0.4 fusion.12
  281.9 0.4 fusion.10
  282.3 1.0 pad_maximum_fusion
  (67 shorter events, 1.9 us)
Async XLA Ops:
  6.5 43.5 %reduce-scatter.2.cloned.1.call-start = ((), (), s32[]{:S(2)}) async-start(), calls=%async_computation.1 | async-start | bytes 884736 | tf_op jit(solution)/shard_map/reduce_scatter | solution.py:61
  14.1 125.5 %all-reduce.13.cloned.1.call-start = ((), (), s32[]{:S(2)}) async-start(), calls=%async_computation.5 | async-start | bytes 1966080 | tf_op jit(solution)/shard_map/psum | solution.py:12
  51.6 17.4 %copy-start.4 = (f32[6,32,256]{2,1,0:T(8,128)}, f32[6,32,256]{2,1,0:T(8,128)S(1)}, u32[]{:S(2)}) copy-start(f32[6,32,256]{2,1,0:T(8,128)S(1)} %fusion.108) | copy-start | bytes 589828
  68.0 122.2 %copy-start.5 = (s32[2,256]{1,0:T(2,128)S(1)}, s32[2,256]{1,0:T(2,128)}, u32[]{:S(2)}) copy-start(s32[2,256]{1,0:T(2,128)} %param.11) | copy-start | bytes 6148
  68.0 122.2 %copy-start.6 = (f32[2,256]{1,0:T(2,128)S(1)}, f32[2,256]{1,0:T(2,128)}, u32[]{:S(2)}) copy-start(f32[2,256]{1,0:T(2,128)} %param.10) | copy-start | bytes 6148
  68.0 122.3 %copy-start.7 = (f32[2,256]{1,0:T(2,128)S(1)}, f32[2,256]{1,0:T(2,128)}, u32[]{:S(2)}) copy-start(f32[2,256]{1,0:T(2,128)} %param.9) | copy-start | bytes 6148
  69.0 120.4 %all-reduce.11.cloned.1.call-start = ((), (), s32[]{:S(2)}) async-start(), calls=%async_computation.2 | async-start | bytes 393216 | tf_op jit(solution)/shard_map/psum | solution.py:13
  139.7 81.4 %all-gather.3.cloned.1.call-start = ((), (), s32[]{:S(2)}) async-start(), calls=%async_computation.3 | async-start | bytes 1769472 | tf_op jit(solution)/shard_map/all_gather | solution.py:77
  189.5 74.9 %all-gather.5.cloned.1.call-start = ((), (), s32[]{:S(2)}) async-start(), calls=%async_computation.4 | async-start | bytes 3932160 | tf_op jit(solution)/shard_map/all_gather | solution.py:64
  222.6 1.0 copy-start.1
  226.3 1.2 copy-start
  268.8 1.0 copy-start.2
  275.2 1.5 copy-start.3
Sparse Core Ops, SparseCore 0:
  14.2 35.8 reduce-scatter.1
  69.2 70.4 all-reduce.12
  142.0 47.4 all-reduce.10
  191.1 29.8 all-gather.2
  222.7 41.6 all-gather.4
